TPU v7x, 256 devices: a whole 4x4x8 slice. The times are simulated.
256 devices in a mesh: grp: 8 (over y, core), sub: 32 (over x, z).
Axes of the slice: x: 4, y: 4, z: 8, core: 2. Of those that a mesh axis runs over, the one named last changes fastest.
Arguments:
- cluster_pos: float32 [3, 4096], P(None, 'sub'), may hold values from -3 to 3
- cluster_vel: float32 [3, 4096], P(None, 'sub'), may hold values from -15 to 15
- cluster_mass: float32 [4096], P('sub'), may hold values from 3 to 60
- galaxy_pos: float32 [3, 131072], P(None, ('grp', 'sub')), may hold values from -1 to 7
- galaxy_vel: float32 [3, 131072], P(None, ('grp', 'sub')), may hold values from -3 to 3
- galaxy_kind: int32 [131072], P(('grp', 'sub')), may hold values from 0 to 3
- species_mass: float32 [4], replicated, may hold values from 10 to 80
Outputs:
- cluster_pos_out: float32 [3, 4096], P(None, 'sub')
- cluster_vel_out: float32 [3, 4096], P(None, 'sub')
- galaxy_pos_out: float32 [3, 131072], P(None, ('grp', 'sub'))
- galaxy_vel_out: float32 [3, 131072], P(None, ('grp', 'sub'))
All inputs are finite; a program needn't handle non-finite values.
Results may differ from a plain program's by a relative error of at most 0.0003.
Values sent between devices are 32-bit elements; how exact they have to be, the bound alone decides.
A program may use at most 64 MiB of HBM per device.

v0:
```python
import jax
import jax.numpy as jnp
from jax import lax
from jax.sharding import PartitionSpec as P

SUBSTEPS = 8
step_time = 0.5
bridge_soft = 0.01
cluster_soft = 0.0025
tile_limit = 524288


def pick_block(target_count, source_count):
    tile_size = target_count
    while tile_size > 1 and (
        tile_size * source_count > tile_limit or target_count % tile_size != 0
    ):
        tile_size = tile_size // 2
    return tile_size


def field(targets, sources, masses, soften):
    target_count = targets.shape[1]
    tile_size = pick_block(target_count, sources.shape[1])

    def field_one_tile(target_tile):
        separation = sources[:, None, :] - target_tile[:, :, None]
        distance = jnp.sum(separation * separation, axis=0) + soften
        inverse = lax.rsqrt(distance)
        weight = masses[None, :] * inverse * inverse * inverse
        return jnp.sum(separation * weight[None], axis=2)

    stacked = targets.reshape(3, target_count // tile_size, tile_size).transpose(1, 0, 2)
    result = lax.map(field_one_tile, stacked)
    return result.transpose(1, 0, 2).reshape(3, target_count)


def rates(target_pos, target_vel, source_pos, source_vel, masses, soften):
    target_count = target_pos.shape[1]
    tile_size = pick_block(target_count, source_pos.shape[1])

    def rates_one_tile(target_tile):
        separation = source_pos[:, None, :] - target_tile[:3, :, None]
        closing = source_vel[:, None, :] - target_tile[3:, :, None]
        distance = jnp.sum(separation * separation, axis=0) + soften
        inverse = lax.rsqrt(distance)
        weight = masses[None, :] * inverse * inverse * inverse
        radial = 3.0 * jnp.sum(separation * closing, axis=0) / distance
        acceleration = jnp.sum(separation * weight[None], axis=2)
        jerk_rate = jnp.sum((closing - radial[None] * separation) * weight[None], axis=2)
        return jnp.concatenate([acceleration, jerk_rate], axis=0)

    stacked = jnp.concatenate([target_pos, target_vel], axis=0)
    stacked = stacked.reshape(6, target_count // tile_size, tile_size).transpose(1, 0, 2)
    result = lax.map(rates_one_tile, stacked)
    return result.transpose(1, 0, 2).reshape(6, target_count)


def local(
    cluster_pos, cluster_vel, cluster_mass, galaxy_pos, galaxy_vel, galaxy_kind, species_mass
):
    star_count = cluster_pos.shape[1]
    member_count = lax.axis_size("sub")
    group_count = lax.axis_size("grp")
    total_stars = star_count * member_count
    total_bodies = galaxy_pos.shape[1] * member_count * group_count
    star_mass = cluster_mass / total_stars
    species = jnp.arange(species_mass.shape[0], dtype=jnp.int32)
    body_mass = (
        jnp.sum(
            jnp.where(galaxy_kind[None, :] == species[:, None], species_mass[:, None], 0.0), axis=0
        )
        / total_bodies
    )
    half_step = step_time / 2.0

    def kick(star_positions, body_positions):
        stacked = jnp.concatenate([star_positions, star_mass[None, :]], axis=0)
        gathered = lax.all_gather(stacked, "sub", axis=1, tiled=True)
        galaxy_push = field(body_positions, gathered[:3], gathered[3], bridge_soft)
        partial_value = field(gathered[:3], body_positions, body_mass, bridge_soft)
        summed = lax.psum(partial_value, ("grp", "sub"))
        cluster_pull = lax.dynamic_slice_in_dim(
            summed, lax.axis_index("sub") * star_count, star_count, 1
        )
        return (cluster_pull, galaxy_push)

    def evaluate(guess_pos, guess_vel):
        sources = jnp.concatenate([guess_pos, guess_vel, star_mass[None, :]], axis=0)
        target_pos, target_vel = (guess_pos, guess_vel)
        source_piece = lax.all_gather(sources, "sub", axis=1, tiled=True)
        result = rates(
            target_pos,
            target_vel,
            source_piece[:3],
            source_piece[3:6],
            source_piece[6],
            cluster_soft,
        )
        return (result[:3], result[3:])

    first_pull, first_push = kick(cluster_pos, galaxy_pos)
    star_vel = cluster_vel + half_step * first_pull
    body_vel = galaxy_vel + half_step * first_push
    body_pos = galaxy_pos + step_time * body_vel
    substep_time = step_time / SUBSTEPS
    positions, velocity = (cluster_pos, star_vel)
    acceleration, jerk_rate = evaluate(positions, velocity)
    for substep in range(SUBSTEPS):
        guess_pos = positions + substep_time * (
            velocity + substep_time * (acceleration / 2.0 + substep_time * jerk_rate / 6.0)
        )
        guess_vel = velocity + substep_time * (acceleration + substep_time * jerk_rate / 2.0)
        new_acc, new_jerk = evaluate(guess_pos, guess_vel)
        new_vel = (
            velocity
            + substep_time / 2.0 * (acceleration + new_acc)
            + substep_time * substep_time / 12.0 * (jerk_rate - new_jerk)
        )
        new_pos = (
            positions
            + substep_time / 2.0 * (velocity + new_vel)
            + substep_time * substep_time / 12.0 * (acceleration - new_acc)
        )
        positions, velocity, acceleration, jerk_rate = (new_pos, new_vel, new_acc, new_jerk)
    second_pull, second_push = kick(positions, body_pos)
    return (
        positions,
        velocity + half_step * second_pull,
        body_pos,
        body_vel + half_step * second_push,
    )


def solution(mesh):
    return jax.shard_map(
        local,
        mesh=mesh,
        in_specs=(
            P(None, "sub"),
            P(None, "sub"),
            P("sub"),
            P(None, ("grp", "sub")),
            P(None, ("grp", "sub")),
            P(("grp", "sub")),
            P(),
        ),
        out_specs=(
            P(None, "sub"),
            P(None, "sub"),
            P(None, ("grp", "sub")),
            P(None, ("grp", "sub")),
        ),
        check_vma=False,
    )
```

profile of v0, /device:TPU:1, one launch (start us, length us, event | category | flops | bytes accessed | tf_op | source)
XLA Modules:
  0.0 715.4 jit_solution(4176489332510097580)
XLA Ops:
  2.0 40.5 %all_gather.33 = f32[4,4096]{1,0:T(4,128)S(1)} all-gather(f32[4,128]{1,0:T(4,128)S(1)} %pad_maximum_fusion.10), channel_id=1, replica_groups=mesh['grp'=8,'sub'=32] {'sub'}, dimensions={1}, use_global_device_ids=true | all-gather | bytes 67584 | tf_op jit(solution)/shard_map/all_gather | solution.py:79
  43.3 14.5 %while.8 = (s32[]{:T(128)}, f32[4,3,1024]{2,1,0:T(4,128)S(1)}, f32[3,512]{1,0:T(4,128)}, f32[4,3,1024]{2,1,0:T(4,128)S(1)}, f32[512]{0:T(512)S(1)}, /*index=5*/s32[]{:T(128)}) while((s32[]{:T(128)}, f32[4,3,1024]{2,1,0:T(4,128)S(1)}, f32[3,512]{1,0:T(4,128)}, f32[4,3,1024]{2,1,0:T(4,128)S(1)}, f32[512]{0:T(512)S(1)}, ...), condition=%wide.region_4.5_spmd, body=%wide.region_1.4_spmd.sunk | while | flops 11006978 | bytes 8521833 | solution.py:34
  57.8 87.6 %psum.14 = f32[3,4096]{1,0:T(4,128)S(1)} all-reduce(f32[3,4096]{1,0:T(4,128)S(1)} %bitcast.93), channel_id=1, replica_groups=mesh['grp'=8,'sub'=32] {'grp','sub'}, use_global_device_ids=true, to_apply=%region_5.6 | all-reduce | flops 12288 | bytes 98304 | tf_op jit(solution)/shard_map/psum | solution.py:82
  145.4 31.0 %all_gather.34 = f32[7,4096]{1,0:T(8,128)S(1)} all-gather(f32[7,128]{1,0:T(8,128)S(1)} %pad_maximum_fusion.8), channel_id=1, replica_groups=mesh['grp'=8,'sub'=32] {'sub'}, dimensions={1}, use_global_device_ids=true | all-gather | bytes 118272 | tf_op jit(solution)/shard_map/all_gather | solution.py:91
  181.2 32.3 %all_gather.35 = f32[7,4096]{1,0:T(8,128)S(1)} all-gather(f32[7,128]{1,0:T(8,128)S(1)} %pad_maximum_fusion.7), channel_id=1, replica_groups=mesh['grp'=8,'sub'=32] {'sub'}, dimensions={1}, use_global_device_ids=true | all-gather | bytes 118272 | tf_op jit(solution)/shard_map/all_gather | solution.py:91
  216.2 2.2 fusion.11
  218.4 31.8 %all_gather.36 = f32[7,4096]{1,0:T(8,128)S(1)} all-gather(f32[7,128]{1,0:T(8,128)S(1)} %pad_maximum_fusion.6), channel_id=1, replica_groups=mesh['grp'=8,'sub'=32] {'sub'}, dimensions={1}, use_global_device_ids=true | all-gather | bytes 118272 | tf_op jit(solution)/shard_map/all_gather | solution.py:91
  252.9 2.2 fusion.13
  255.1 33.7 %all_gather.37 = f32[7,4096]{1,0:T(8,128)S(1)} all-gather(f32[7,128]{1,0:T(8,128)S(1)} %pad_maximum_fusion.5), channel_id=1, replica_groups=mesh['grp'=8,'sub'=32] {'sub'}, dimensions={1}, use_global_device_ids=true | all-gather | bytes 118272 | tf_op jit(solution)/shard_map/all_gather | solution.py:91
  291.5 2.2 fusion.15
  293.7 30.9 %all_gather.38 = f32[7,4096]{1,0:T(8,128)S(1)} all-gather(f32[7,128]{1,0:T(8,128)S(1)} %pad_maximum_fusion.4), channel_id=1, replica_groups=mesh['grp'=8,'sub'=32] {'sub'}, dimensions={1}, use_global_device_ids=true | all-gather | bytes 118272 | tf_op jit(solution)/shard_map/all_gather | solution.py:91
  327.3 2.2 fusion.17
  329.5 33.5 %all_gather.39 = f32[7,4096]{1,0:T(8,128)S(1)} all-gather(f32[7,128]{1,0:T(8,128)S(1)} %pad_maximum_fusion.3), channel_id=1, replica_groups=mesh['grp'=8,'sub'=32] {'sub'}, dimensions={1}, use_global_device_ids=true | all-gather | bytes 118272 | tf_op jit(solution)/shard_map/all_gather | solution.py:91
  365.7 2.2 fusion.19
  367.9 30.7 %all_gather.40 = f32[7,4096]{1,0:T(8,128)S(1)} all-gather(f32[7,128]{1,0:T(8,128)S(1)} %pad_maximum_fusion.2), channel_id=1, replica_groups=mesh['grp'=8,'sub'=32] {'sub'}, dimensions={1}, use_global_device_ids=true | all-gather | bytes 118272 | tf_op jit(solution)/shard_map/all_gather | solution.py:91
  401.3 2.2 fusion.21
  403.5 33.4 %all_gather.41 = f32[7,4096]{1,0:T(8,128)S(1)} all-gather(f32[7,128]{1,0:T(8,128)S(1)} %pad_maximum_fusion.1), channel_id=1, replica_groups=mesh['grp'=8,'sub'=32] {'sub'}, dimensions={1}, use_global_device_ids=true | all-gather | bytes 118272 | tf_op jit(solution)/shard_map/all_gather | solution.py:91
  439.6 2.2 fusion.23
  441.8 31.1 %all_gather.42 = f32[7,4096]{1,0:T(8,128)S(1)} all-gather(f32[7,128]{1,0:T(8,128)S(1)} %pad_maximum_fusion), channel_id=1, replica_groups=mesh['grp'=8,'sub'=32] {'sub'}, dimensions={1}, use_global_device_ids=true | all-gather | bytes 118272 | tf_op jit(solution)/shard_map/all_gather | solution.py:91
  477.9 36.5 %all_gather.43 = f32[4,4096]{1,0:T(4,128)S(1)} all-gather(f32[4,128]{1,0:T(4,128)S(1)} %pad_maximum_fusion.9), channel_id=1, replica_groups=mesh['grp'=8,'sub'=32] {'sub'}, dimensions={1}, use_global_device_ids=true | all-gather | bytes 67584 | tf_op jit(solution)/shard_map/all_gather | solution.py:79
  514.4 8.5 %while.9 = (s32[]{:T(128)}, f32[4,3,128]{2,1,0:T(4,128)S(1)}, f32[3,4096]{1,0:T(4,128)S(1)}, f32[4,3,128]{2,1,0:T(4,128)S(1)}, f32[1,4096]{1,0:T(1,128)S(1)}, /*index=5*/s32[]{:T(128)}) while((s32[]{:T(128)}, f32[4,3,128]{2,1,0:T(4,128)S(1)}, f32[3,4096]{1,0:T(4,128)S(1)}, f32[4,3,128]{2,1,0:T(4,128)S(1)}, f32[1,4096]{1,0:T(1,128)S(1)}, ...), condition=%wide.region_45.46_spmd, body=%wide.region_42.45_spmd.sunk | while | flops 11009666 | bytes 8515149 | solution.py:34
  523.0 8.5 %while.11 = (s32[]{:T(128)}, f32[4,3,128]{2,1,0:T(4,128)S(1)}, f32[3,4096]{1,0:T(4,128)S(1)}, f32[4,3,128]{2,1,0:T(4,128)S(1)}, f32[1,4096]{1,0:T(1,128)S(1)}, /*index=5*/s32[]{:T(128)}) while((s32[]{:T(128)}, f32[4,3,128]{2,1,0:T(4,128)S(1)}, f32[3,4096]{1,0:T(4,128)S(1)}, f32[4,3,128]{2,1,0:T(4,128)S(1)}, f32[1,4096]{1,0:T(1,128)S(1)}, ...), condition=%wide.region_54.55_spmd, body=%wide.region_51.54_spmd.sunk | while | flops 11009666 | bytes 8515149 | solution.py:34
  532.1 10.4 %while.10 = (s32[]{:T(128)}, f32[4,3,1024]{2,1,0:T(4,128)S(1)}, f32[3,512]{1,0:T(4,128)S(1)}, f32[4,3,1024]{2,1,0:T(4,128)S(1)}, f32[512]{0:T(512)S(1)}, /*index=5*/s32[]{:T(128)}) while((s32[]{:T(128)}, f32[4,3,1024]{2,1,0:T(4,128)S(1)}, f32[3,512]{1,0:T(4,128)S(1)}, f32[4,3,1024]{2,1,0:T(4,128)S(1)}, f32[512]{0:T(512)S(1)}, ...), condition=%wide.region_49.50_spmd, body=%wide.region_46.49_spmd.sunk | while | flops 11006978 | bytes 8497229 | solution.py:34
  542.5 171.9 %psum.15 = f32[3,4096]{1,0:T(4,128)S(1)} all-reduce(f32[3,4096]{1,0:T(4,128)S(1)} %bitcast.92), channel_id=1, replica_groups=mesh['grp'=8,'sub'=32] {'grp','sub'}, use_global_device_ids=true, to_apply=%region_50.51 | all-reduce | flops 12288 | bytes 98304 | tf_op jit(solution)/shard_map/psum | solution.py:82
  (174 shorter events, 72.9 us)
Async XLA Ops:
  43.2 102.1 %copy-start.6 = (f32[3,128]{1,0:T(4,128)S(1)}, f32[3,128]{1,0:T(4,128)}, u32[]{:S(2)}) copy-start(f32[3,128]{1,0:T(4,128)} %param.16) | copy-start | bytes 4612
  43.2 102.1 %copy-start.3 = (f32[3,128]{1,0:T(4,128)S(1)}, f32[3,128]{1,0:T(4,128)}, u32[]{:S(2)}) copy-start(f32[3,128]{1,0:T(4,128)} %param.15) | copy-start | bytes 4612
  44.9 0.7 copy-start
  48.6 0.7 copy-start
  52.2 0.7 copy-start
  55.8 0.7 copy-start
  475.6 38.8 %copy-start.1 = (f32[3,512]{1,0:T(4,128)S(1)}, f32[3,512]{1,0:T(4,128)}, u32[]{:S(2)}) copy-start(f32[3,512]{1,0:T(4,128)} %get-tuple-element.607) | copy-start | bytes 18436
  477.8 36.6 %copy-start.5 = (f32[3,128]{1,0:T(4,128)}, f32[3,128]{1,0:T(4,128)S(1)}, u32[]{:S(2)}) copy-start(f32[3,128]{1,0:T(4,128)S(1)} %multiply_add_fusion.2) | copy-start | bytes 4612
  514.4 8.5 %copy-start.4 = (f32[3,512]{1,0:T(4,128)S(1)}, f32[3,512]{1,0:T(4,128)}, u32[]{:S(2)}) copy-start(f32[3,512]{1,0:T(4,128)} %param.19) | copy-start | bytes 18436
  542.5 172.5 %copy-start.2 = (f32[3,512]{1,0:T(4,128)}, f32[3,512]{1,0:T(4,128)S(1)}, u32[]{:S(2)}) copy-start(f32[3,512]{1,0:T(4,128)S(1)} %get-tuple-element.610) | copy-start | bytes 18436
where the time goes:
time: 725 us; the launch traced here: 715 us
  blocking collectives  625 us (86%)
  other arithmetic  86 us (12%)
    all_gather x9, blocking collectives, evaluate(): source_piece = lax.all_gather(sources, 'sub', axis=1, tiled=True)  288 us
    psum x2, blocking collectives, kick(): summed = lax.psum(partial_value, ('grp', 'sub'))  259 us
    all_gather x2, blocking collectives, kick(): gathered = lax.all_gather(stacked, 'sub', axis=1, tiled=True)  76.9 us
    reduce_sum x8, other arithmetic, rates_one_tile(): jnp.sum((closing - radial[None] * separation) * weight[None], axis=2)  17.5 us
    reduce_sum x16, other arithmetic, field_one_tile(): distance = jnp.sum(separation * separation, axis=0) + soften  17.3 us
    reduce_sum x16, other arithmetic, field_one_tile(): return jnp.sum(separation * weight[None], axis=2)  16.5 us
    reduce_sum x8, other arithmetic, rates_one_tile(): radial = 3.0 * jnp.sum(separation * closing, axis=0) / distance  16.4 us

commit v1 on v0

--- a/solution.py
+++ b/solution.py
@@ -76,7 +76,8 @@
 
     def kick(star_positions, body_positions):
         stacked = jnp.concatenate([star_positions, star_mass[None, :]], axis=0)
-        gathered = lax.all_gather(stacked, "sub", axis=1, tiled=True)
+        stack = jnp.stack([stacked] * lax.axis_size("sub"))
+        gathered = jnp.concatenate(lax.all_to_all(stack, "sub", 0, 0), axis=1)
         galaxy_push = field(body_positions, gathered[:3], gathered[3], bridge_soft)
         partial_value = field(gathered[:3], body_positions, body_mass, bridge_soft)
         summed = lax.psum(partial_value, ("grp", "sub"))

time: 725 us -> 661 us (0.912)
  blocking collectives: 625 us -> 526 us
  waiting for transfers between devices: 0 us -> 16.9 us
  starting transfers between devices: 0 us -> 16.6 us
    all_gather x2 -> x0, blocking collectives: 76.9 us -> none  [kick(): gathered = lax.all_gather(stacked, 'sub', axis=1, tiled=True)]
    psum x2, blocking collectives: 259 us -> 236 us  [kick(): summed = lax.psum(partial_value, ('grp', 'sub'))]
    all_to_all x0 -> x2, waiting for transfers between devices: none -> 16.9 us  [kick(): gathered = jnp.concatenate(lax.all_to_all(stack, 'sub', 0, 0), axis=1)]
    all_to_all x0 -> x2, starting transfers between devices: none -> 16.6 us  [kick(): gathered = jnp.concatenate(lax.all_to_all(stack, 'sub', 0, 0), axis=1)]
  transfers between devices with their start and end apart: 0 -> 2, of which waited for: 0 -> 2; matrix products, arithmetic and copies ran while one was open for 0% -> 0% of each run, Pallas kernels for 0% -> 0%
where the time goes in v1:
time: 661 us; the launch traced here: 651 us
  blocking collectives  526 us (80%)
  other arithmetic  86.1 us (13%)
  waiting for transfers between devices  16.9 us (3%)
  starting transfers between devices  16.6 us (3%)
    all_gather x9, blocking collectives, evaluate(): source_piece = lax.all_gather(sources, 'sub', axis=1, tiled=True)  290 us
    psum x2, blocking collectives, kick(): summed = lax.psum(partial_value, ('grp', 'sub'))  236 us
    reduce_sum x8, other arithmetic, rates_one_tile(): jnp.sum((closing - radial[None] * separation) * weight[None], axis=2)  17.6 us
    reduce_sum x16, other arithmetic, field_one_tile(): distance = jnp.sum(separation * separation, axis=0) + soften  17.3 us
    all_to_all x2, waiting for transfers between devices, kick(): gathered = jnp.concatenate(lax.all_to_all(stack, 'sub', 0, 0), axis=1)  16.9 us
    all_to_all x2, starting transfers between devices, kick(): gathered = jnp.concatenate(lax.all_to_all(stack, 'sub', 0, 0), axis=1)  16.6 us
    reduce_sum x16, other arithmetic, field_one_tile(): return jnp.sum(separation * weight[None], axis=2)  16.6 us
    reduce_sum x8, other arithmetic, rates_one_tile(): radial = 3.0 * jnp.sum(separation * closing, axis=0) / distance  16.4 us
  transfers between devices with their start and end apart: 2, of which 2 were waited for; matrix products, arithmetic and copies ran while one was open for 0% of the time, Pallas kernels for 0%

profile of v1, /device:TPU:1, one launch (start us, length us, event | category | flops | bytes accessed | tf_op | source)
XLA Modules:
  0.0 651.4 jit_solution(15166992775129627120)
XLA Ops:
  2.6 11.9 %all-to-all-start = ((f32[32,4,128]{2,1,0:T(4,128)}), f32[32,4,128]{2,1,0:T(4,128)S(1)}, u32[]{:S(2)}, u32[]{:S(2)}) async-start(f32[32,4,128]{2,1,0:T(4,128)} %stack.4), calls=%async_computation | async-start | bytes 131072 | tf_op jit(solution)/shard_map/all_to_all | solution.py:80
  15.3 8.1 %all-to-all-done = f32[32,4,128]{2,1,0:T(4,128)S(1)} async-done(((f32[32,4,128]{2,1,0:T(4,128)}), f32[32,4,128]{2,1,0:T(4,128)S(1)}, u32[]{:S(2)}, u32[]{:S(2)}) %all-to-all-start) | async-done | bytes 65568 | tf_op jit(solution)/shard_map/all_to_all | solution.py:80
  23.5 14.6 %while.8 = (s32[]{:T(128)}, f32[4,3,1024]{2,1,0:T(4,128)S(1)}, f32[3,512]{1,0:T(4,128)}, f32[4,3,1024]{2,0,1:T(4,128)S(1)}, f32[512]{0:T(512)S(1)}, /*index=5*/s32[]{:T(128)}) while((s32[]{:T(128)}, f32[4,3,1024]{2,1,0:T(4,128)S(1)}, f32[3,512]{1,0:T(4,128)}, f32[4,3,1024]{2,0,1:T(4,128)S(1)}, f32[512]{0:T(512)S(1)}, ...), condition=%wide.region_4.5_spmd, body=%wide.region_1.4_spmd.sunk | while | flops 11006978 | bytes 8546417 | solution.py:34
  38.0 75.6 %psum.14 = f32[3,4096]{1,0:T(4,128)S(1)} all-reduce(f32[3,4096]{1,0:T(4,128)S(1)} %bitcast.102), channel_id=1, replica_groups=mesh['grp'=8,'sub'=32] {'grp','sub'}, use_global_device_ids=true, to_apply=%region_5.6 | all-reduce | flops 12288 | bytes 98304 | tf_op jit(solution)/shard_map/psum | solution.py:83
  113.7 32.0 %all_gather.27 = f32[7,4096]{1,0:T(8,128)S(1)} all-gather(f32[7,128]{1,0:T(8,128)S(1)} %pad_maximum_fusion.8), channel_id=1, replica_groups=mesh['grp'=8,'sub'=32] {'sub'}, dimensions={1}, use_global_device_ids=true | all-gather | bytes 118272 | tf_op jit(solution)/shard_map/all_gather | solution.py:92
  150.4 31.4 %all_gather.28 = f32[7,4096]{1,0:T(8,128)S(1)} all-gather(f32[7,128]{1,0:T(8,128)S(1)} %pad_maximum_fusion.7), channel_id=1, replica_groups=mesh['grp'=8,'sub'=32] {'sub'}, dimensions={1}, use_global_device_ids=true | all-gather | bytes 118272 | tf_op jit(solution)/shard_map/all_gather | solution.py:92
  184.5 2.2 fusion.11
  186.7 33.0 %all_gather.29 = f32[7,4096]{1,0:T(8,128)S(1)} all-gather(f32[7,128]{1,0:T(8,128)S(1)} %pad_maximum_fusion.6), channel_id=1, replica_groups=mesh['grp'=8,'sub'=32] {'sub'}, dimensions={1}, use_global_device_ids=true | all-gather | bytes 118272 | tf_op jit(solution)/shard_map/all_gather | solution.py:92
  222.4 2.2 fusion.13
  224.7 31.7 %all_gather.30 = f32[7,4096]{1,0:T(8,128)S(1)} all-gather(f32[7,128]{1,0:T(8,128)S(1)} %pad_maximum_fusion.5), channel_id=1, replica_groups=mesh['grp'=8,'sub'=32] {'sub'}, dimensions={1}, use_global_device_ids=true | all-gather | bytes 118272 | tf_op jit(solution)/shard_map/all_gather | solution.py:92
  259.1 2.2 fusion.15
  261.3 32.7 %all_gather.31 = f32[7,4096]{1,0:T(8,128)S(1)} all-gather(f32[7,128]{1,0:T(8,128)S(1)} %pad_maximum_fusion.4), channel_id=1, replica_groups=mesh['grp'=8,'sub'=32] {'sub'}, dimensions={1}, use_global_device_ids=true | all-gather | bytes 118272 | tf_op jit(solution)/shard_map/all_gather | solution.py:92
  298.9 31.3 %all_gather.32 = f32[7,4096]{1,0:T(8,128)S(1)} all-gather(f32[7,128]{1,0:T(8,128)S(1)} %pad_maximum_fusion.3), channel_id=1, replica_groups=mesh['grp'=8,'sub'=32] {'sub'}, dimensions={1}, use_global_device_ids=true | all-gather | bytes 118272 | tf_op jit(solution)/shard_map/all_gather | solution.py:92
  332.9 2.2 fusion.19
  335.1 32.5 %all_gather.33 = f32[7,4096]{1,0:T(8,128)S(1)} all-gather(f32[7,128]{1,0:T(8,128)S(1)} %pad_maximum_fusion.2), channel_id=1, replica_groups=mesh['grp'=8,'sub'=32] {'sub'}, dimensions={1}, use_global_device_ids=true | all-gather | bytes 118272 | tf_op jit(solution)/shard_map/all_gather | solution.py:92
  372.5 31.7 %all_gather.34 = f32[7,4096]{1,0:T(8,128)S(1)} all-gather(f32[7,128]{1,0:T(8,128)S(1)} %pad_maximum_fusion.1), channel_id=1, replica_groups=mesh['grp'=8,'sub'=32] {'sub'}, dimensions={1}, use_global_device_ids=true | all-gather | bytes 118272 | tf_op jit(solution)/shard_map/all_gather | solution.py:92
  409.2 33.6 %all_gather.35 = f32[7,4096]{1,0:T(8,128)S(1)} all-gather(f32[7,128]{1,0:T(8,128)S(1)} %pad_maximum_fusion), channel_id=1, replica_groups=mesh['grp'=8,'sub'=32] {'sub'}, dimensions={1}, use_global_device_ids=true | all-gather | bytes 118272 | tf_op jit(solution)/shard_map/all_gather | solution.py:92
  442.8 8.5 %while.9 = (s32[]{:T(128)}, f32[4,3,128]{2,1,0:T(4,128)S(1)}, f32[3,4096]{1,0:T(4,128)S(1)}, f32[4,3,128]{2,1,0:T(4,128)S(1)}, f32[1,4096]{1,0:T(1,128)S(1)}, /*index=5*/s32[]{:T(128)}) while((s32[]{:T(128)}, f32[4,3,128]{2,1,0:T(4,128)S(1)}, f32[3,4096]{1,0:T(4,128)S(1)}, f32[4,3,128]{2,1,0:T(4,128)S(1)}, f32[1,4096]{1,0:T(1,128)S(1)}, ...), condition=%wide.region_45.46_spmd, body=%wide.region_42.45_spmd.sunk | while | flops 11009666 | bytes 8515157 | solution.py:34
  454.0 2.3 fusion.25
  456.9 4.7 all-to-all-start.1
  461.7 8.8 %all-to-all-done.1 = f32[32,4,128]{2,1,0:T(4,128)S(1)} async-done(((f32[32,4,128]{2,1,0:T(4,128)}), f32[32,4,128]{2,1,0:T(4,128)S(1)}, u32[]{:S(2)}, u32[]{:S(2)}) %all-to-all-start.1) | async-done | bytes 65568 | tf_op jit(solution)/shard_map/all_to_all | solution.py:80
  470.6 8.5 %while.11 = (s32[]{:T(128)}, f32[4,3,128]{2,1,0:T(4,128)S(1)}, f32[3,4096]{1,0:T(4,128)S(1)}, f32[4,3,128]{2,1,0:T(4,128)S(1)}, f32[1,4096]{1,0:T(1,128)S(1)}, /*index=5*/s32[]{:T(128)}) while((s32[]{:T(128)}, f32[4,3,128]{2,1,0:T(4,128)S(1)}, f32[3,4096]{1,0:T(4,128)S(1)}, f32[4,3,128]{2,1,0:T(4,128)S(1)}, f32[1,4096]{1,0:T(1,128)S(1)}, ...), condition=%wide.region_54.55_spmd, body=%wide.region_51.54_spmd.sunk | while | flops 11009666 | bytes 8515157 | solution.py:34
  479.8 10.5 %while.10 = (s32[]{:T(128)}, f32[4,3,1024]{2,1,0:T(4,128)S(1)}, f32[3,512]{1,0:T(4,128)S(1)}, f32[4,3,1024]{2,0,1:T(4,128)S(1)}, f32[512]{0:T(512)S(1)}, /*index=5*/s32[]{:T(128)}) while((s32[]{:T(128)}, f32[4,3,1024]{2,1,0:T(4,128)S(1)}, f32[3,512]{1,0:T(4,128)S(1)}, f32[4,3,1024]{2,0,1:T(4,128)S(1)}, f32[512]{0:T(512)S(1)}, ...), condition=%wide.region_49.50_spmd, body=%wide.region_46.49_spmd.sunk | while | flops 11006978 | bytes 8521813 | solution.py:34
  490.3 160.1 %psum.15 = f32[3,4096]{1,0:T(4,128)S(1)} all-reduce(f32[3,4096]{1,0:T(4,128)S(1)} %bitcast.101), channel_id=1, replica_groups=mesh['grp'=8,'sub'=32] {'grp','sub'}, use_global_device_ids=true, to_apply=%region_50.51 | all-reduce | flops 12288 | bytes 98304 | tf_op jit(solution)/shard_map/psum | solution.py:83
  (192 shorter events, 78.8 us)
Async XLA Ops:
  2.6 20.7 %all-to-all-start = ((f32[32,4,128]{2,1,0:T(4,128)}), f32[32,4,128]{2,1,0:T(4,128)S(1)}, u32[]{:S(2)}, u32[]{:S(2)}) async-start(f32[32,4,128]{2,1,0:T(4,128)} %stack.4), calls=%async_computation | async-start | bytes 131072 | tf_op jit(solution)/shard_map/all_to_all | solution.py:80
  23.4 90.2 %copy-start.6 = (f32[3,128]{1,0:T(4,128)S(1)}, f32[3,128]{1,0:T(4,128)}, u32[]{:S(2)}) copy-start(f32[3,128]{1,0:T(4,128)} %param.16) | copy-start | bytes 4612
  23.5 90.2 %copy-start.3 = (f32[3,128]{1,0:T(4,128)S(1)}, f32[3,128]{1,0:T(4,128)}, u32[]{:S(2)}) copy-start(f32[3,128]{1,0:T(4,128)} %param.15) | copy-start | bytes 4612
  25.2 0.7 copy-start
  28.8 0.7 copy-start
  32.4 0.7 copy-start
  36.1 0.7 copy-start
  407.0 35.9 %copy-start.1 = (f32[3,512]{1,0:T(4,128)S(1)}, f32[3,512]{1,0:T(4,128)}, u32[]{:S(2)}) copy-start(f32[3,512]{1,0:T(4,128)} %get-tuple-element.639) | copy-start | bytes 18436
  454.0 7.7 %copy-start.4 = (f32[3,512]{1,0:T(4,128)S(1)}, f32[3,512]{1,0:T(4,128)}, u32[]{:S(2)}) copy-start(f32[3,512]{1,0:T(4,128)} %param.19) | copy-start | bytes 18436
  456.3 14.3 %copy-start.5 = (f32[3,128]{1,0:T(4,128)}, f32[3,128]{1,0:T(4,128)S(1)}, u32[]{:S(2)}) copy-start(f32[3,128]{1,0:T(4,128)S(1)} %multiply_add_fusion.2) | copy-start | bytes 4612
  456.9 13.6 %all-to-all-start.1 = ((f32[32,4,128]{2,1,0:T(4,128)}), f32[32,4,128]{2,1,0:T(4,128)S(1)}, u32[]{:S(2)}, u32[]{:S(2)}) async-start(f32[32,4,128]{2,1,0:T(4,128)} %stack.5), calls=%async_computation.1 | async-start | bytes 131072 | tf_op jit(solution)/shard_map/all_to_all | solution.py:80
  490.3 160.7 %copy-start.2 = (f32[3,512]{1,0:T(4,128)}, f32[3,512]{1,0:T(4,128)S(1)}, u32[]{:S(2)}) copy-start(f32[3,512]{1,0:T(4,128)S(1)} %get-tuple-element.642) | copy-start | bytes 18436
